TPU v7x, 32 devices: a whole 2x2x4 slice. The times are simulated.
32 devices in a mesh: lon: 8 (over z, x), lat: 4 (over y, core).
Axes of the slice: x: 2, y: 2, z: 4, core: 2. Of those that a mesh axis runs over, the one named last changes fastest.
Arguments:
- courant: float32 [4, 2, 137, 32, 512], P(None, None, None, 'lon', 'lat'), may hold values from -0.45 to 0.45
- slot_column_cells: int32 [4, 32, 32, 4], P(None, ('lon', 'lat')), may hold values from 0 to 511
- column_counts: int32 [4, 32, 32], P(None, ('lon', 'lat')), may hold values from 1 to 4, as said below
- innovations: float32 [4, 32, 32, 4, 128], P(None, ('lon', 'lat')), may hold values from -6 to 6
- error_weight: float32 [4, 32, 32, 4, 128], P(None, ('lon', 'lat')), may hold values from 0.3 to 3
- weighting: float32 [274, 128], replicated, may hold values from -0.375 to 0.375
Outputs:
- solution: float32 [2, 137, 32, 512], P(None, None, 'lon', 'lat')
- residual: float32 [2, 137, 32, 512], P(None, None, 'lon', 'lat')
Inputs may be any that keep to these rules, and one draw needn't show every extreme that they name: `slot_column_cells`: A cell of the sending device's block, numbered longitude-major over its 4 x 128 cells; only slots below the matching count are read. `column_counts`: at every timestep some owner receives 4 live slots from every sending device.
All inputs are finite; a program needn't handle non-finite values.
Results may differ from a plain program's by a relative error of at most 0.00016.
Values sent between devices are 32-bit elements; how exact they have to be, the bound alone decides.
A program may use at most 128 MiB of HBM per device.

v0:
```python
import functools

import jax
import jax.numpy as jnp
from jax import lax
from jax.experimental import pallas as pl
from jax.experimental.pallas import tpu as pltpu
from jax.sharding import PartitionSpec as P

ITERS = 2
CHUNKS = 4
TILE = 24
MESH = pl.DeviceIdType.MESH
F32 = jnp.float32
BF16 = jnp.bfloat16


def split(value):
    high = value.astype(BF16)
    return high, (value - high.astype(F32)).astype(BF16)


def dot(a, b):
    return jnp.dot(a, b, preferred_element_type=F32)


def dot_nt(a, b):
    return lax.dot_general(a, b, (((1,), (1,)), ((), ())), preferred_element_type=F32)


def kernel(
    lon_n, lat_n, valid,
    courant, cells, scale, target, up_w, down_w,
    x_out, r_out,
    p, s, dep, y_acc, v_dep, onehot, seen,
    snd, rcv, part1, part2, sums1, sums2,
    ssem, rsem, s1, r1, s2, r2,
):
    times, _, slab, levels, band = courant.shape
    chan = up_w.shape[1]
    rows_h = 2 * levels // CHUNKS
    per_var = levels // rows_h
    a = lax.axis_index("lon")
    b = lax.axis_index("lat")
    peers = (
        (lax.rem(a + lon_n - 1, lon_n), b),
        (lax.rem(a + 1, lon_n), b),
        (a, lax.rem(b + lat_n - 1, lat_n)),
        (a, lax.rem(b + 1, lat_n)),
    )

    for par in range(2):
        for d in range(4):
            for var in range(2):
                tail = slice(var * levels + valid // 8 * 8, (var + 1) * levels)
                rcv[par, d, tail, :] = jnp.zeros((levels - valid // 8 * 8, band), F32)
    barrier = pltpu.get_barrier_semaphore()
    for off in range(1, lon_n):
        pl.semaphore_signal(barrier, inc=1, device_id=(lax.rem(a + off, lon_n), b), device_id_type=MESH)
    for off in range(1, lat_n):
        pl.semaphore_signal(barrier, inc=1, device_id=(a, lax.rem(b + off, lat_n)), device_id_type=MESH)

    lane = lax.broadcasted_iota(jnp.int32, (TILE, band), 1)
    has_south = (b > 0).astype(F32)
    has_north = (b < lat_n - 1).astype(F32)
    cols = [slice(i * band, (i + 1) * band) for i in range(slab)]

    def copies(par, h):
        span = pl.ds(h * rows_h, min(rows_h, valid - (h % per_var) * rows_h))
        return [
            pltpu.make_async_remote_copy(
                src_ref=snd.at[par, d, span],
                dst_ref=rcv.at[par, d, span],
                send_sem=ssem.at[par, h, d],
                recv_sem=rsem.at[par, h, d],
                device_id=peers[d],
                device_id_type=MESH,
            )
            for d in range(4)
        ]

    def start(par, h):
        for copy in copies(par, h):
            copy.start()

    def wait(par, h):
        for copy in copies(par, h):
            copy.wait()

    def tiles(h, body, carry=None):
        for n in range(rows_h // TILE):
            row = pl.ds(h * rows_h + n * TILE, TILE)
            crow = pl.ds((h % per_var) * rows_h + n * TILE, TILE)
            carry = body(row, crow, carry)
        return carry

    def winds(t, crow):
        return (
            [courant[t, 0, i, crow, :] for i in range(slab)],
            [courant[t, 1, i, crow, :] for i in range(slab)],
        )

    def load(ref, row):
        return [ref[row, c] for c in cols]

    def store(ref, row, values):
        for c, value in zip(cols, values):
            ref[row, c] = value

    def turn(value, shift):
        shift = shift % band
        return value if shift == 0 else pltpu.roll(value, shift, 1)

    def halos(par, row):
        from_south = rcv[par, 3, row, :] * has_south
        from_north = rcv[par, 2, row, :] * has_north
        return rcv[par, 1, row, :], rcv[par, 0, row, :], from_south, from_north

    def shifted(value, halo, i, up):
        if up:
            return jnp.where(lane == 0, turn(halo, -i), turn(value, 1))
        return jnp.where(lane == band - 1, turn(halo, slab - 1 - i), turn(value, -1))

    def advance(t, row, crow, par):
        u, v = winds(t, crow)
        x = load(s, row)
        west, east, south, north = halos(par, row)
        full = [west] + x + [east]
        outs = []
        for i in range(slab):
            out = (1.0 - jnp.abs(u[i]) - jnp.abs(v[i])) * x[i]
            out += jnp.maximum(u[i], 0.0) * full[i]
            out += jnp.maximum(-u[i], 0.0) * full[i + 2]
            out += jnp.maximum(v[i], 0.0) * shifted(x[i], south, i, True)
            out += jnp.maximum(-v[i], 0.0) * shifted(x[i], north, i, False)
            outs.append(out)
        return outs

    def retreat(t, row, crow, par):
        u, v = winds(t, crow)
        y = load(s, row)
        west, east, south, north = halos(par, row)
        plus = [jnp.maximum(u[i], 0.0) * y[i] for i in range(slab)] + [east]
        minus = [west] + [jnp.maximum(-u[i], 0.0) * y[i] for i in range(slab)]
        outs = []
        for i in range(slab):
            out = (1.0 - jnp.abs(u[i]) - jnp.abs(v[i])) * y[i]
            out += plus[i + 1] + minus[i]
            out += shifted(jnp.maximum(v[i], 0.0) * y[i], north, i, False)
            out += shifted(jnp.maximum(-v[i], 0.0) * y[i], south, i, True)
            outs.append(out)
        return outs

    def put_edges(par, row, west, east, southward, northward):
        snd[par, 0, row, :] = west
        snd[par, 1, row, :] = east
        low = jnp.zeros((TILE, band), F32)
        high = low
        for i in range(slab):
            low = jnp.where(lane == band - slab + i, turn(southward[i], band - slab + i), low)
            high = jnp.where(lane == i, turn(northward[i], i + 1), high)
        snd[par, 2, row, :] = low
        snd[par, 3, row, :] = high

    def put_state(par, row, x):
        put_edges(par, row, x[0], x[-1], x, x)

    def put_products(par, t, row, crow, y):
        u, v = winds(t, crow)
        put_edges(
            par, row,
            jnp.maximum(u[0], 0.0) * y[0],
            jnp.maximum(-u[-1], 0.0) * y[-1],
            [jnp.maximum(v[i], 0.0) * y[i] for i in range(slab)],
            [jnp.maximum(-v[i], 0.0) * y[i] for i in range(slab)],
        )

    def project(var):
        high, low = split(s[var * levels : (var + 1) * levels, :])
        y = dot(up_w[var], jnp.concatenate([high, high, low], axis=0))
        if var == 0:
            y_acc[...] = y
        else:
            y_acc[...] += y

    def scatter(t, weigh):
        pair = jnp.concatenate(split(weigh(t)), axis=0)
        both = dot_nt(pair, onehot[t])
        high, low = split(both[:chan] + both[chan:])
        v_dep[:chan, :] = high
        v_dep[chan : 2 * chan, :] = high
        v_dep[2 * chan :, :] = low

    def observe(k, t):
        pair = jnp.concatenate(split(y_acc[...]), axis=0)
        both = dot(pair, onehot[t])
        seen[k, t] = both[:chan] + both[chan:]

    def deposit(var, into):
        span = slice(var * levels, (var + 1) * levels)
        into[span, :] = dot(down_w[span, :], v_dep[...])

    def adjoint(weigh, finish, carry, pass_on, slot=None, partials=None):
        scatter(times - 1, weigh)
        for var in range(2):
            deposit(var, s)
            for h in range(var * per_var, (var + 1) * per_var):
                def enter(row, crow, none):
                    put_products(0, times - 1, row, crow, load(s, row))

                tiles(h, enter)
                start(0, h)
        if slot is not None:
            first_leg(slot, *partials())

        def step(n, none):
            t = times - 1 - n
            par = lax.rem(n, 2)
            scatter(t - 1, weigh)
            for var in range(2):
                deposit(var, dep)
            if slot is not None:
                @pl.when(n == 1)
                def _():
                    second_leg(slot)

            for h in range(CHUNKS):
                wait(par, h)

                def back(row, crow, none):
                    y = [v + d for v, d in zip(retreat(t, row, crow, par), load(dep, row))]
                    store(s, row, y)
                    put_products(1 - par, t - 1, row, crow, y)

                tiles(h, back)
                start(1 - par, h)
            return none

        lax.fori_loop(0, times - 1, step, 0)
        if slot is not None:
            finish = finish(*totals(slot))
        par = (times - 1) % 2
        for h in range(CHUNKS):
            wait(par, h)

            def last(row, crow, carry):
                return finish(row, retreat(0, row, crow, par), carry)

            carry = tiles(h, last, carry)
            if pass_on:
                start(0, h)
        return carry

    def tangent(k, slot=None):
        def step(t, none):
            par = lax.rem(t, 2)
            if slot is not None:
                @pl.when(t == 1)
                def _():
                    second_leg(slot)

            for h in range(CHUNKS):
                wait(par, h)

                def onward(row, crow, none):
                    x = advance(t, row, crow, par)
                    store(s, row, x)
                    put_state(1 - par, row, x)

                tiles(h, onward)
                start(1 - par, h)
                if (h + 1) % per_var == 0:
                    project(h // per_var)
            observe(k, t)
            return none

        lax.fori_loop(0, times - 1, step, 0)
        par = (times - 1) % 2
        for h in range(CHUNKS):
            wait(par, h)

            def last(row, crow, none):
                store(s, row, advance(times - 1, row, crow, par))

            tiles(h, last)
            if (h + 1) % per_var == 0:
                project(h // per_var)
        observe(k, times - 1)

    def legs(k, axis):
        count, me, source, sums, send, receive = (
            (lon_n, a, part1, sums1, s1, r1),
            (lat_n, b, part2, sums2, s2, r2),
        )[axis]
        moves = []
        for off in range(1, count):
            other = lax.rem(me + off, count)
            moves.append(
                pltpu.make_async_remote_copy(
                    src_ref=source.at[k],
                    dst_ref=sums.at[k, me],
                    send_sem=send.at[k, off - 1],
                    recv_sem=receive.at[k, off - 1],
                    device_id=(other, b) if axis == 0 else (a, other),
                    device_id_type=MESH,
                )
            )
        return moves

    def launch(k, axis, tile):
        source, sums, me = ((part1, sums1, a), (part2, sums2, b))[axis]
        source[k] = tile
        sums[k, me] = tile
        for move in legs(k, axis):
            move.start()

    def land(k, axis):
        for move in legs(k, axis):
            move.wait()
        sums, count = ((sums1, lon_n), (sums2, lat_n))[axis]
        total = sums[k, 0]
        for j in range(1, count):
            total = total + sums[k, j]
        return total

    def first_leg(k, first, second):
        launch(k, 0, jnp.concatenate([first, second], axis=0))

    def second_leg(k):
        launch(k, 1, land(k, 0))

    def totals(k):
        tile = land(k, 1)
        return [jnp.sum(tile[8 * n : 8 * n + 8], keepdims=True) for n in range(2)]

    def fold(value):
        return value.reshape(TILE // 8, 8, band).sum(0)

    slots = cells.shape[-1]
    place = lax.broadcasted_iota(jnp.int32, (slab * band, slots), 0)
    for t in range(times):
        here = jnp.broadcast_to(cells[t], (slab * band, slots))
        onehot[t] = jnp.where(here == place, 1.0, 0.0).astype(BF16)
    pl.semaphore_wait(barrier, lon_n + lat_n - 2)

    zero = jnp.zeros((8, band), F32)

    def begin(row, values, acc):
        put_state(0, row, values)
        for value in values:
            acc = acc + fold(value * value)
        store(s, row, values)
        store(p, row, values)
        return acc

    def norm(value):
        value = value.reshape(-1, 8, value.shape[-1]).sum(0)
        width = value.shape[-1]
        return sum(value[:, i : i + band] for i in range(0, width, band))

    def weigh_first(t):
        return scale[t] * seen[0, t]

    acc = adjoint(lambda t: target[t], begin, zero, True)
    tangent(0)
    scalars = []

    def energy_first():
        total = zero
        for t in range(times):
            total = total + norm(weigh_first(t) * seen[0, t])
        return acc, total

    def imager(rho, energy):
        scalars.extend([rho, energy])

        def image(row, values, qq):
            outs = []
            for d, value in zip(load(p, row), values):
                q = d + value
                outs.append(q)
                qq = qq + fold(q * q)
            put_state(0, row, outs)
            store(s, row, outs)
            store(r_out, row, outs)
            return qq

        return image

    qq = adjoint(weigh_first, imager, zero, True, 0, energy_first)
    first_leg(1, qq, zero)
    tangent(1, 1)
    rho, energy = scalars
    qq = totals(1)[0]
    pq = rho + energy
    alpha = rho / pq
    rho_new = rho - 2.0 * alpha * pq + alpha * alpha * qq
    beta = rho_new / rho
    grown = 1.0 + beta
    square = rho_new + beta * beta * rho

    def seen_next(t):
        return grown * seen[0, t] - alpha * seen[1, t]

    def weigh_next(t):
        return scale[t] * seen_next(t)

    def energy_next():
        total = zero
        for t in range(times):
            y = seen_next(t)
            total = total + norm(scale[t] * y * y)
        return total, zero

    def closer(energy, none):
        step = rho_new / (square + energy)

        def close(row, values, carry):
            first = load(p, row)
            image = load(r_out, row)
            d = [grown * v - alpha * q for v, q in zip(first, image)]
            store(x_out, row, [alpha * v + step * w for v, w in zip(first, d)])
            residual = [v - alpha * q for v, q in zip(first, image)]
            store(r_out, row, [v - step * (w + z) for v, w, z in zip(residual, d, values)])
            return carry

        return close

    adjoint(weigh_next, closer, 0, False, 2, energy_next)


def pair_of(value):
    high = lax.reduce_precision(value, 8, 7)
    return high, lax.reduce_precision(value - high, 8, 7)


def body(courant, slot_column_cells, column_counts, innovations, error_weight, weighting):
    times, _, levels, slab, band = courant.shape
    owners, cap = slot_column_cells.shape[2:]
    chan = weighting.shape[1]
    slots = owners * cap
    lon_n, lat_n = lax.axis_size("lon"), lax.axis_size("lat")
    deep = -(-levels // 48) * 48

    field = jnp.pad(courant.transpose(0, 1, 3, 2, 4), ((0, 0),) * 3 + ((0, deep - levels), (0, 0)))
    weights = jnp.pad(weighting.reshape(2, levels, chan), ((0, 0), (0, deep - levels), (0, 0)))
    high, low = pair_of(weights)
    down_w = jnp.concatenate([high, low, high], axis=2).reshape(2 * deep, 3 * chan).astype(BF16)
    up_w = jnp.concatenate([high, low, high], axis=1).transpose(0, 2, 1).astype(BF16)
    here = error_weight[:, 0]
    both = jnp.stack([here, here * innovations[:, 0]]).transpose(2, 0, 1, 3, 4)
    both = lax.all_to_all(both, ("lon", "lat"), split_axis=0, concat_axis=0, tiled=True)
    position = lax.broadcasted_iota(jnp.int32, (times, owners, cap), 2)
    live = (position < column_counts[:, 0][:, :, None]).astype(F32).reshape(times, 1, slots)
    both = both.transpose(1, 2, 4, 0, 3).reshape(2, times, chan, slots) * live
    cells = slot_column_cells[:, 0].reshape(times, 1, slots)

    state = (2 * deep, slab * band)
    vmem = pl.BlockSpec(memory_space=pltpu.VMEM)
    sums = 3
    x, r = pl.pallas_call(
        functools.partial(kernel, lon_n, lat_n, levels),
        out_shape=[jax.ShapeDtypeStruct(state, F32)] * 2,
        in_specs=[vmem] * 6,
        out_specs=[vmem] * 2,
        scratch_shapes=[
            pltpu.VMEM(state, F32),
            pltpu.VMEM(state, F32),
            pltpu.VMEM(state, F32),
            pltpu.VMEM((chan, slab * band), F32),
            pltpu.VMEM((3 * chan, slab * band), BF16),
            pltpu.VMEM((times, slab * band, slots), BF16),
            pltpu.VMEM((ITERS, times, chan, slots), F32),
            pltpu.VMEM((2, 4, 2 * deep, band), F32),
            pltpu.VMEM((2, 4, 2 * deep, band), F32),
            pltpu.VMEM((sums, 16, band), F32),
            pltpu.VMEM((sums, 16, band), F32),
            pltpu.VMEM((sums, lon_n, 16, band), F32),
            pltpu.VMEM((sums, lat_n, 16, band), F32),
            pltpu.SemaphoreType.DMA((2, CHUNKS, 4)),
            pltpu.SemaphoreType.DMA((2, CHUNKS, 4)),
            pltpu.SemaphoreType.DMA((sums, lon_n - 1)),
            pltpu.SemaphoreType.DMA((sums, lon_n - 1)),
            pltpu.SemaphoreType.DMA((sums, lat_n - 1)),
            pltpu.SemaphoreType.DMA((sums, lat_n - 1)),
        ],
        compiler_params=pltpu.CompilerParams(collective_id=0, has_side_effects=True, vmem_limit_bytes=48 * 2**20),
    )(field, cells, both[0], both[1], up_w, down_w)

    def back(state):
        return state.reshape(2, deep, slab, band)[:, :levels]

    return back(x), back(r)


def solution(mesh):
    owned = ("lon", "lat")
    in_specs = (
        P(None, None, None, "lon", "lat"),
        P(None, owned, None, None),
        P(None, owned, None),
        P(None, owned, None, None, None),
        P(None, owned, None, None, None),
        P(),
    )
    out_specs = (P(None, None, "lon", "lat"), P(None, None, "lon", "lat"))
    return jax.shard_map(body, mesh=mesh, in_specs=in_specs, out_specs=out_specs, check_vma=False)
```

profile of v0, /device:TPU:0, one launch (start us, length us, event | category | flops | bytes accessed | tf_op | source)
XLA Modules:
  0.0 167.2 jit_solution(17099191448092620876)
XLA Ops:
  0.6 0.0 copy-start.1
  0.6 1.1 copy.33
  1.8 1.1 bitcast_multiply_fusion
  2.9 0.9 maximum_bitcast_fusion
  3.8 7.3 %all-to-all-start = ((f32[32,2,4,4,128]{4,3,2,1,0:T(4,128)}), f32[32,2,4,4,128]{4,3,2,1,0:T(4,128)S(1)}, u32[]{:S(2)}, u32[]{:S(2)}) async-start(f32[32,2,4,4,128]{4,3,2,1,0:T(4,128)} %maximum_bitcast_fusion), calls=%async_computation | async-start | bytes 1048576 | tf_op jit(solution)/shard_map/all_to_all | solution.py:452
  11.1 0.0 copy-done.1
  11.2 0.0 copy-start.5
  11.2 0.0 copy-start.6
  11.2 0.0 copy-start.4
  11.2 1.6 copy.32
  12.8 0.0 copy-done.5
  12.8 0.1 copy.19
  12.9 0.1 reshape_squeeze.3
  13.0 0.1 lt.17
  13.1 0.1 lt.18
  13.2 0.1 iota.12
  13.3 0.1 copy.24
  13.5 0.0 copy-start.2
  13.5 0.6 copy-done.2
  14.2 0.2 copy.25
  14.4 0.0 copy-start.3
  14.4 1.9 %pad.8.courant = f32[4,2,4,144,128]{4,3,2,1,0:T(8,128)S(1)} pad(f32[4,2,4,137,128]{4,3,2,1,0:T(8,128)} %bitcast.29, f32[]{:T(128)} %constant.2.clone.1), padding=0_0x0_0x0_0x0_7x0_0 | pad | bytes 4603908 | tf_op jit(solution)/shard_map/jit(_pad)/pad | solution.py:445
  16.3 0.2 maximum_bitcast_fusion.1.up_w
  16.5 10.2 %all-to-all-done = f32[32,2,4,4,128]{4,3,2,1,0:T(4,128)S(1)} async-done(((f32[32,2,4,4,128]{4,3,2,1,0:T(4,128)}), f32[32,2,4,4,128]{4,3,2,1,0:T(4,128)S(1)}, u32[]{:S(2)}, u32[]{:S(2)}) %all-to-all-start) | async-done | bytes 524320 | tf_op jit(solution)/shard_map/all_to_all | solution.py:452
  26.8 0.9 copy.22
  27.7 1.2 copy.23
  29.0 134.2 %shard_map.77 = (f32[288,512]{1,0:T(8,128)S(1)}, f32[288,512]{1,0:T(8,128)S(1)}) custom-call(f32[4,2,4,144,128]{4,3,2,1,0:T(8,128)S(1)} %pad.8.courant, s32[4,1,128]{2,1,0:T(1,128)S(1)} %bitcast.28, f32[4,128,128]{2,1,0:T(8,128)S(1)} %get-tuple-element.7.scale, f32[4,128,128]{2,1,0:T(8,128)S(1)} %get-tuple-element.6.target, ...), custom_call_target="tpu_custom_call" | custom-call | tf_op jit(solution)/shard_map/pallas_call | solution.py:461
  163.2 0.8 copy-done
  164.0 1.3 reshape.55
  165.3 0.8 slice.18
  166.1 0.2 reshape.56
  166.4 0.8 slice.19
  (11 shorter events, 0.2 us)
Async XLA Ops:
  0.6 10.5 %copy-start.1 = (f32[4,2,137,4,128]{4,3,2,1,0:T(4,128)S(1)}, f32[4,2,137,4,128]{4,3,2,1,0:T(4,128)}, u32[]{:S(2)}) copy-start(f32[4,2,137,4,128]{4,3,2,1,0:T(4,128)} %param.6) | copy-start | bytes 6733828
  3.8 22.9 %all-to-all-start = ((f32[32,2,4,4,128]{4,3,2,1,0:T(4,128)}), f32[32,2,4,4,128]{4,3,2,1,0:T(4,128)S(1)}, u32[]{:S(2)}, u32[]{:S(2)}) async-start(f32[32,2,4,4,128]{4,3,2,1,0:T(4,128)} %maximum_bitcast_fusion), calls=%async_computation | async-start | bytes 1048576 | tf_op jit(solution)/shard_map/all_to_all | solution.py:452
  11.2 1.6 copy-start.5
  11.2 1.8 %copy-start.6 = (s32[4,1,32]{2,1,0:T(1,128)S(1)}, s32[4,1,32]{2,1,0:T(1,128)}, u32[]{:S(2)}) copy-start(s32[4,1,32]{2,1,0:T(1,128)} %param.8) | copy-start | bytes 1540
  11.2 2.1 %copy-start.4 = (f32[274,128]{1,0:T(8,128)S(1)}, f32[274,128]{1,0:T(8,128)}, u32[]{:S(2)}) copy-start(f32[274,128]{1,0:T(8,128)} %param.11) | copy-start | bytes 420868
  13.5 0.7 copy-start.2
  14.4 1.9 %copy-start.3 = (bf16[2,144,128]{1,2,0:T(8,128)(2,1)S(1)}, bf16[2,144,128]{1,2,0:T(8,128)(2,1)}, u32[]{:S(2)}) copy-start(bf16[2,144,128]{1,2,0:T(8,128)(2,1)} %copy-done.2) | copy-start | bytes 221188
  163.2 0.8 copy-start
where the time goes:
time: 168 us; the launch traced here: 167 us
  Pallas kernels  134 us (80%)
  local copies, waits for them, and re-layouts  12.2 us (7%)
  waiting for transfers between devices  10.2 us (6%)
  starting transfers between devices  7.33 us (4%)
  other arithmetic  2.3 us (1%)
    pallas_call x1, Pallas kernels, body(): pl.pallas_call(functools.partial(kernel, lon_n, lat_n, levels), out_shape...  134 us
    all_to_all x1, waiting for transfers between devices, body(): lax.all_to_all(both, ('lon', 'lat'), split_axis=0, concat_axis=0, tiled=T...  10.2 us
    all_to_all x1, starting transfers between devices, body(): lax.all_to_all(both, ('lon', 'lat'), split_axis=0, concat_axis=0, tiled=T...  7.33 us
    unnamed x17, local copies, waits for them, and re-layouts  4.32 us
  transfers between devices with their start and end apart: 1, of which 1 were waited for; matrix products, arithmetic and copies ran while one was open for 3% of the time, Pallas kernels for 0%

commit v1 on v0

--- a/solution.py
+++ b/solution.py
@@ -30,13 +30,15 @@
 
 def kernel(
     lon_n, lat_n, valid,
-    courant, cells, scale, target, up_w, down_w,
+    raw, cells, live, innovations, weights, up_w, down_w,
     x_out, r_out,
-    p, s, dep, y_acc, v_dep, onehot, seen,
+    courant, scale, target, sent, came, heavy,
+    p, s, keep, dep, y_acc, v_dep, onehot, seen,
     snd, rcv, part1, part2, sums1, sums2,
-    ssem, rsem, s1, r1, s2, r2,
+    ssem, rsem, s1, r1, s2, r2, asem, bsem,
 ):
     times, _, slab, levels, band = courant.shape
+    count, cap = sent.shape[1:3]
     chan = up_w.shape[1]
     rows_h = 2 * levels // CHUNKS
     per_var = levels // rows_h
@@ -54,11 +56,19 @@
             for var in range(2):
                 tail = slice(var * levels + valid // 8 * 8, (var + 1) * levels)
                 rcv[par, d, tail, :] = jnp.zeros((levels - valid // 8 * 8, band), F32)
+    me = a * lat_n + b
+
+    def place_of(off):
+        other = lax.rem(me + off, count)
+        return other, (other // lat_n, lax.rem(other, lat_n))
+
     barrier = pltpu.get_barrier_semaphore()
-    for off in range(1, lon_n):
-        pl.semaphore_signal(barrier, inc=1, device_id=(lax.rem(a + off, lon_n), b), device_id_type=MESH)
-    for off in range(1, lat_n):
-        pl.semaphore_signal(barrier, inc=1, device_id=(a, lax.rem(b + off, lat_n)), device_id_type=MESH)
+
+    def greet(off, none):
+        pl.semaphore_signal(barrier, inc=1, device_id=place_of(off)[1], device_id_type=MESH)
+        return none
+
+    lax.fori_loop(1, count, greet, 0)
 
     lane = lax.broadcasted_iota(jnp.int32, (TILE, band), 1)
     has_south = (b > 0).astype(F32)
@@ -333,6 +343,36 @@
         tile = land(k, 1)
         return [jnp.sum(tile[8 * n : 8 * n + 8], keepdims=True) for n in range(2)]
 
+    def parcel(which, source, landing, off):
+        other, device = place_of(off)
+        return pltpu.make_async_remote_copy(
+            src_ref=source.at[:, other],
+            dst_ref=landing.at[:, me],
+            send_sem=asem.at[which, off - 1],
+            recv_sem=bsem.at[which, off - 1],
+            device_id=device,
+            device_id_type=MESH,
+        )
+
+    def post(which, source, landing):
+        landing[:, me] = source[:, me]
+
+        def one(off, none):
+            parcel(which, source, landing, off).start()
+            return none
+
+        lax.fori_loop(1, count, one, 0)
+
+    def collect(which, source, landing, into):
+        def one(off, none):
+            parcel(which, source, landing, off).wait()
+            return none
+
+        lax.fori_loop(1, count, one, 0)
+        for t in range(times):
+            rows = jnp.concatenate([landing[t, :, c, :] for c in range(cap)], axis=0)
+            into[t] = rows.T * live[t]
+
     def fold(value):
         return value.reshape(TILE // 8, 8, band).sum(0)
 
@@ -341,7 +381,23 @@
     for t in range(times):
         here = jnp.broadcast_to(cells[t], (slab * band, slots))
         onehot[t] = jnp.where(here == place, 1.0, 0.0).astype(BF16)
-    pl.semaphore_wait(barrier, lon_n + lat_n - 2)
+    for t in range(times):
+        sent[t] = weights[t] * innovations[t]
+    pl.semaphore_wait(barrier, count - 1)
+    post(0, sent, came)
+    whole = valid // 8 * 8
+    for t in range(times):
+        for c in range(2):
+            for i in range(slab):
+                base = (t * 2 + c) * valid * slab + i
+                for level in range(0, whole, 8):
+                    courant[t, c, i, level : level + 8, :] = raw[pl.ds(base + level * slab, 8, stride=slab), :]
+                courant[t, c, i, whole:, :] = jnp.zeros((levels - whole, band), F32)
+                for level in range(whole, valid):
+                    row = base + level * slab
+                    courant[t, c, i, level : level + 1, :] = raw[row : row + 1, :]
+    collect(0, sent, came, target)
+    post(1, weights, heavy)
 
     zero = jnp.zeros((8, band), F32)
 
@@ -362,6 +418,7 @@
         return scale[t] * seen[0, t]
 
     acc = adjoint(lambda t: target[t], begin, zero, True)
+    collect(1, weights, heavy, scale)
     tangent(0)
     scalars = []
 
@@ -382,7 +439,7 @@
                 qq = qq + fold(q * q)
             put_state(0, row, outs)
             store(s, row, outs)
-            store(r_out, row, outs)
+            store(keep, row, outs)
             return qq
 
         return image
@@ -412,16 +469,27 @@
             total = total + norm(scale[t] * y * y)
         return total, zero
 
+    def put_out(ref, row, values):
+        var, level = divmod(row.start, levels)
+        for low in range(0, TILE, 8):
+            here = min(8, valid - level - low)
+            for i, value in enumerate(values):
+                base = (var * valid + level + low) * slab + i
+                if here > 1:
+                    ref[pl.ds(base, here, stride=slab), :] = value[low : low + here]
+                elif here == 1:
+                    ref[base : base + 1, :] = value[low : low + 1]
+
     def closer(energy, none):
         step = rho_new / (square + energy)
 
         def close(row, values, carry):
             first = load(p, row)
-            image = load(r_out, row)
+            image = load(keep, row)
             d = [grown * v - alpha * q for v, q in zip(first, image)]
-            store(x_out, row, [alpha * v + step * w for v, w in zip(first, d)])
+            put_out(x_out, row, [alpha * v + step * w for v, w in zip(first, d)])
             residual = [v - alpha * q for v, q in zip(first, image)]
-            store(r_out, row, [v - step * (w + z) for v, w, z in zip(residual, d, values)])
+            put_out(r_out, row, [v - step * (w + z) for v, w, z in zip(residual, d, values)])
             return carry
 
         return close
@@ -442,28 +510,32 @@
     lon_n, lat_n = lax.axis_size("lon"), lax.axis_size("lat")
     deep = -(-levels // 48) * 48
 
-    field = jnp.pad(courant.transpose(0, 1, 3, 2, 4), ((0, 0),) * 3 + ((0, deep - levels), (0, 0)))
+    field = courant.reshape(-1, band)
     weights = jnp.pad(weighting.reshape(2, levels, chan), ((0, 0), (0, deep - levels), (0, 0)))
     high, low = pair_of(weights)
     down_w = jnp.concatenate([high, low, high], axis=2).reshape(2 * deep, 3 * chan).astype(BF16)
     up_w = jnp.concatenate([high, low, high], axis=1).transpose(0, 2, 1).astype(BF16)
-    here = error_weight[:, 0]
-    both = jnp.stack([here, here * innovations[:, 0]]).transpose(2, 0, 1, 3, 4)
-    both = lax.all_to_all(both, ("lon", "lat"), split_axis=0, concat_axis=0, tiled=True)
-    position = lax.broadcasted_iota(jnp.int32, (times, owners, cap), 2)
-    live = (position < column_counts[:, 0][:, :, None]).astype(F32).reshape(times, 1, slots)
-    both = both.transpose(1, 2, 4, 0, 3).reshape(2, times, chan, slots) * live
-    cells = slot_column_cells[:, 0].reshape(times, 1, slots)
+    position = lax.broadcasted_iota(jnp.int32, (times, cap, owners), 1)
+    live = (position < column_counts[:, 0][:, None, :]).astype(F32).reshape(times, 1, slots)
+    cells = slot_column_cells[:, 0].transpose(0, 2, 1).reshape(times, 1, slots)
+    mail = (times, owners, cap, chan)
 
     state = (2 * deep, slab * band)
     vmem = pl.BlockSpec(memory_space=pltpu.VMEM)
     sums = 3
     x, r = pl.pallas_call(
         functools.partial(kernel, lon_n, lat_n, levels),
-        out_shape=[jax.ShapeDtypeStruct(state, F32)] * 2,
-        in_specs=[vmem] * 6,
+        out_shape=[jax.ShapeDtypeStruct((2 * levels * slab, band), F32)] * 2,
+        in_specs=[vmem] * 7,
         out_specs=[vmem] * 2,
         scratch_shapes=[
+            pltpu.VMEM((times, 2, slab, deep, band), F32),
+            pltpu.VMEM((times, chan, slots), F32),
+            pltpu.VMEM((times, chan, slots), F32),
+            pltpu.VMEM(mail, F32),
+            pltpu.VMEM(mail, F32),
+            pltpu.VMEM(mail, F32),
+            pltpu.VMEM(state, F32),
             pltpu.VMEM(state, F32),
             pltpu.VMEM(state, F32),
             pltpu.VMEM(state, F32),
@@ -483,12 +555,14 @@
             pltpu.SemaphoreType.DMA((sums, lon_n - 1)),
             pltpu.SemaphoreType.DMA((sums, lat_n - 1)),
             pltpu.SemaphoreType.DMA((sums, lat_n - 1)),
+            pltpu.SemaphoreType.DMA((2, owners - 1)),
+            pltpu.SemaphoreType.DMA((2, owners - 1)),
         ],
         compiler_params=pltpu.CompilerParams(collective_id=0, has_side_effects=True, vmem_limit_bytes=48 * 2**20),
-    )(field, cells, both[0], both[1], up_w, down_w)
+    )(field, cells, live, innovations[:, 0], error_weight[:, 0], up_w, down_w)
 
     def back(state):
-        return state.reshape(2, deep, slab, band)[:, :levels]
+        return state.reshape(2, levels, slab, band)
 
     return back(x), back(r)
 

time: 168 us -> 159 us (0.946)
  Pallas kernels: 134 us -> 151 us
  waiting for transfers between devices: 10.2 us -> 0 us
  starting transfers between devices: 7.33 us -> 0 us
  local copies, waits for them, and re-layouts: 12.2 us -> 5.65 us
    pallas_call x1, Pallas kernels: 134 us -> 151 us  [body(): pl.pallas_call(functools.partial(kernel, lon_n, lat_n, levels), out_shape...]
    all_to_all x1 -> x0, waiting for transfers between devices: 10.2 us -> none  [body(): lax.all_to_all(both, ('lon', 'lat'), split_axis=0, concat_axis=0, tiled=T...]
    all_to_all x1 -> x0, starting transfers between devices: 7.33 us -> none  [body(): lax.all_to_all(both, ('lon', 'lat'), split_axis=0, concat_axis=0, tiled=T...]
    unnamed x17 -> x8, local copies, waits for them, and re-layouts: 4.32 us -> 1.63 us
    pad x1 -> x0, local copies, waits for them, and re-layouts: 1.88 us -> none  [body(): jnp.pad(courant.transpose(0, 1, 3, 2, 4), ((0, 0),) * 3 + ((0, deep - lev...]
    reshape x3 -> x1, local copies, waits for them, and re-layouts: 2.69 us -> 0.93 us  [body(): cells = slot_column_cells[:, 0].transpose(0, 2, 1).reshape(times, 1, slots)]
    slice x2 -> x0, local copies, waits for them, and re-layouts: 1.69 us -> none  [back(): return state.reshape(2, deep, slab, band)[:, :levels]]
  transfers between devices with their start and end apart: 1 -> 0, of which waited for: 1 -> 0; matrix products, arithmetic and copies ran while one was open for 3% -> 0% of each run, Pallas kernels for 0% -> 0%
where the time goes in v1:
time: 159 us; the launch traced here: 158 us
  Pallas kernels  151 us (95%)
  local copies, waits for them, and re-layouts  5.65 us (4%)
    pallas_call x1, Pallas kernels, body(): pl.pallas_call(functools.partial(kernel, lon_n, lat_n, levels), out_shape...  151 us

profile of v1, /device:TPU:0, one launch (start us, length us, event | category | flops | bytes accessed | tf_op | source)
XLA Modules:
  0.0 158.3 jit_solution(11459314962337697337)
XLA Ops:
  0.6 0.0 copy-start.2
  0.6 0.0 copy-start.1
  0.7 0.0 copy-start
  0.7 0.9 reshape.60.cells
  1.6 0.1 iota.12
  1.7 0.7 lt.20
  2.4 0.1 lt.21
  2.5 0.9 reshape.61
  3.4 0.1 copy.9
  3.6 0.2 maximum_bitcast_fusion.up_w
  3.7 0.8 pad_maximum_fusion
  4.5 1.2 copy.10
  5.7 0.0 copy-done.2
  5.7 0.0 copy-done.1
  5.7 0.0 copy-done
  5.7 151.0 %shard_map.77 = (f32[1096,128]{1,0:T(8,128)S(1)}, f32[1096,128]{1,0:T(8,128)S(1)}) custom-call(f32[4384,128]{1,0:T(8,128)S(1)} %bitcast.12, s32[4,1,128]{2,1,0:T(1,128)S(1)} %reshape.60.cells, f32[4,1,128]{2,1,0:T(1,128)S(1)} %compare_convert_fusion.live, f32[4,32,4,128]{3,2,1,0:T(4,128)S(1)} %bitcast.16, f32[4,32,4,128]{3,2,1,0:T(4,128)S(1)} %bitcast.17, ...), custom_call_target="tpu_custom_call" | custom-call | tf_op jit(solution)/shard_map/pallas_call | solution.py:526
  156.7 0.8 copy.13
  157.5 0.8 copy.14
  (3 shorter events, 0.0 us)
Async XLA Ops:
  0.6 5.1 %copy-start.2 = (f32[4,1,32,4,128]{4,3,2,1,0:T(4,128)S(1)}, f32[4,1,32,4,128]{4,3,2,1,0:T(4,128)}, u32[]{:S(2)}) copy-start(f32[4,1,32,4,128]{4,3,2,1,0:T(4,128)} %param.10) | copy-start | bytes 786436
  0.6 5.1 %copy-start.1 = (f32[4,1,32,4,128]{4,3,2,1,0:T(4,128)S(1)}, f32[4,1,32,4,128]{4,3,2,1,0:T(4,128)}, u32[]{:S(2)}) copy-start(f32[4,1,32,4,128]{4,3,2,1,0:T(4,128)} %param.9) | copy-start | bytes 786436
  0.7 5.1 %copy-start = (f32[4,2,137,4,128]{4,3,2,1,0:T(4,128)S(1)}, f32[4,2,137,4,128]{4,3,2,1,0:T(4,128)}, u32[]{:S(2)}) copy-start(f32[4,2,137,4,128]{4,3,2,1,0:T(4,128)} %param.6) | copy-start | bytes 6733828

commit v2 on v1

--- a/solution.py
+++ b/solution.py
@@ -30,16 +30,17 @@
 
 def kernel(
     lon_n, lat_n, valid,
-    raw, cells, live, innovations, weights, up_w, down_w,
+    far_raw, cells, live, far_innovations, far_weights, far_weighting,
     x_out, r_out,
-    courant, scale, target, sent, came, heavy,
+    raw, innovations, weights, weighting,
+    courant, scale, target, sent, came, heavy, padded, up_w, down_w,
     p, s, keep, dep, y_acc, v_dep, onehot, seen,
     snd, rcv, part1, part2, sums1, sums2,
-    ssem, rsem, s1, r1, s2, r2, asem, bsem,
+    ssem, rsem, s1, r1, s2, r2, asem, bsem, lsem,
 ):
     times, _, slab, levels, band = courant.shape
     count, cap = sent.shape[1:3]
-    chan = up_w.shape[1]
+    chan = weighting.shape[1]
     rows_h = 2 * levels // CHUNKS
     per_var = levels // rows_h
     a = lax.axis_index("lon")
@@ -56,6 +57,15 @@
             for var in range(2):
                 tail = slice(var * levels + valid // 8 * 8, (var + 1) * levels)
                 rcv[par, d, tail, :] = jnp.zeros((levels - valid // 8 * 8, band), F32)
+    pairs = (
+        (far_innovations, innovations),
+        (far_weights, weights),
+        (far_raw, raw),
+        (far_weighting, weighting),
+    )
+    loads = [pltpu.make_async_copy(src, dst, lsem.at[n]) for n, (src, dst) in enumerate(pairs)]
+    for one in loads:
+        one.start()
     me = a * lat_n + b
 
     def place_of(off):
@@ -210,7 +220,7 @@
         span = slice(var * levels, (var + 1) * levels)
         into[span, :] = dot(down_w[span, :], v_dep[...])
 
-    def adjoint(weigh, finish, carry, pass_on, slot=None, partials=None):
+    def adjoint(weigh, finish, carry, pass_on, slot=None, partials=None, early=None):
         scatter(times - 1, weigh)
         for var in range(2):
             deposit(var, s)
@@ -226,6 +236,8 @@
         def step(n, none):
             t = times - 1 - n
             par = lax.rem(n, 2)
+            if early is not None:
+                pl.when(n == 0)(early)
             scatter(t - 1, weigh)
             for var in range(2):
                 deposit(var, dep)
@@ -343,11 +355,14 @@
         tile = land(k, 1)
         return [jnp.sum(tile[8 * n : 8 * n + 8], keepdims=True) for n in range(2)]
 
+    groups = ((times - 1, 1), (0, times - 1), (0, times))
+
     def parcel(which, source, landing, off):
         other, device = place_of(off)
+        span = pl.ds(*groups[which])
         return pltpu.make_async_remote_copy(
-            src_ref=source.at[:, other],
-            dst_ref=landing.at[:, me],
+            src_ref=source.at[span, other],
+            dst_ref=landing.at[span, me],
             send_sem=asem.at[which, off - 1],
             recv_sem=bsem.at[which, off - 1],
             device_id=device,
@@ -355,7 +370,9 @@
         )
 
     def post(which, source, landing):
-        landing[:, me] = source[:, me]
+        first, length = groups[which]
+        for t in range(first, first + length):
+            landing[t, me] = source[t, me]
 
         def one(off, none):
             parcel(which, source, landing, off).start()
@@ -369,7 +386,8 @@
             return none
 
         lax.fori_loop(1, count, one, 0)
-        for t in range(times):
+        first, length = groups[which]
+        for t in range(first, first + length):
             rows = jnp.concatenate([landing[t, :, c, :] for c in range(cap)], axis=0)
             into[t] = rows.T * live[t]
 
@@ -381,10 +399,23 @@
     for t in range(times):
         here = jnp.broadcast_to(cells[t], (slab * band, slots))
         onehot[t] = jnp.where(here == place, 1.0, 0.0).astype(BF16)
+    loads[0].wait()
+    loads[1].wait()
     for t in range(times):
         sent[t] = weights[t] * innovations[t]
     pl.semaphore_wait(barrier, count - 1)
     post(0, sent, came)
+    post(1, sent, came)
+    loads[2].wait()
+    loads[3].wait()
+    for var in range(2):
+        padded[var] = jnp.zeros((levels, chan), F32)
+        padded[var, :valid, :] = weighting[var * valid : (var + 1) * valid, :]
+        high, low = split(padded[var])
+        for n, part in enumerate((high, low, high)):
+            down_w[var * levels : (var + 1) * levels, n * chan : (n + 1) * chan] = part
+        high, low = split(padded[var].T)
+        up_w[var] = jnp.concatenate([high, low, high], axis=1)
     whole = valid // 8 * 8
     for t in range(times):
         for c in range(2):
@@ -397,7 +428,11 @@
                     row = base + level * slab
                     courant[t, c, i, level : level + 1, :] = raw[row : row + 1, :]
     collect(0, sent, came, target)
-    post(1, weights, heavy)
+
+    def rest():
+        collect(1, sent, came, target)
+        post(2, weights, heavy)
+
 
     zero = jnp.zeros((8, band), F32)
 
@@ -417,8 +452,8 @@
     def weigh_first(t):
         return scale[t] * seen[0, t]
 
-    acc = adjoint(lambda t: target[t], begin, zero, True)
-    collect(1, weights, heavy, scale)
+    acc = adjoint(lambda t: target[t], begin, zero, True, early=rest)
+    collect(2, weights, heavy, scale)
     tangent(0)
     scalars = []
 
@@ -497,11 +532,6 @@
     adjoint(weigh_next, closer, 0, False, 2, energy_next)
 
 
-def pair_of(value):
-    high = lax.reduce_precision(value, 8, 7)
-    return high, lax.reduce_precision(value - high, 8, 7)
-
-
 def body(courant, slot_column_cells, column_counts, innovations, error_weight, weighting):
     times, _, levels, slab, band = courant.shape
     owners, cap = slot_column_cells.shape[2:]
@@ -511,10 +541,6 @@
     deep = -(-levels // 48) * 48
 
     field = courant.reshape(-1, band)
-    weights = jnp.pad(weighting.reshape(2, levels, chan), ((0, 0), (0, deep - levels), (0, 0)))
-    high, low = pair_of(weights)
-    down_w = jnp.concatenate([high, low, high], axis=2).reshape(2 * deep, 3 * chan).astype(BF16)
-    up_w = jnp.concatenate([high, low, high], axis=1).transpose(0, 2, 1).astype(BF16)
     position = lax.broadcasted_iota(jnp.int32, (times, cap, owners), 1)
     live = (position < column_counts[:, 0][:, None, :]).astype(F32).reshape(times, 1, slots)
     cells = slot_column_cells[:, 0].transpose(0, 2, 1).reshape(times, 1, slots)
@@ -522,19 +548,27 @@
 
     state = (2 * deep, slab * band)
     vmem = pl.BlockSpec(memory_space=pltpu.VMEM)
+    far = pl.BlockSpec(memory_space=pltpu.HBM)
     sums = 3
     x, r = pl.pallas_call(
         functools.partial(kernel, lon_n, lat_n, levels),
         out_shape=[jax.ShapeDtypeStruct((2 * levels * slab, band), F32)] * 2,
-        in_specs=[vmem] * 7,
+        in_specs=[far, vmem, vmem, far, far, far],
         out_specs=[vmem] * 2,
         scratch_shapes=[
+            pltpu.VMEM(field.shape, F32),
+            pltpu.VMEM(mail, F32),
+            pltpu.VMEM(mail, F32),
+            pltpu.VMEM(weighting.shape, F32),
             pltpu.VMEM((times, 2, slab, deep, band), F32),
             pltpu.VMEM((times, chan, slots), F32),
             pltpu.VMEM((times, chan, slots), F32),
             pltpu.VMEM(mail, F32),
             pltpu.VMEM(mail, F32),
             pltpu.VMEM(mail, F32),
+            pltpu.VMEM((2, deep, chan), F32),
+            pltpu.VMEM((2, chan, 3 * deep), BF16),
+            pltpu.VMEM((2 * deep, 3 * chan), BF16),
             pltpu.VMEM(state, F32),
             pltpu.VMEM(state, F32),
             pltpu.VMEM(state, F32),
@@ -555,11 +589,12 @@
             pltpu.SemaphoreType.DMA((sums, lon_n - 1)),
             pltpu.SemaphoreType.DMA((sums, lat_n - 1)),
             pltpu.SemaphoreType.DMA((sums, lat_n - 1)),
-            pltpu.SemaphoreType.DMA((2, owners - 1)),
-            pltpu.SemaphoreType.DMA((2, owners - 1)),
+            pltpu.SemaphoreType.DMA((3, owners - 1)),
+            pltpu.SemaphoreType.DMA((3, owners - 1)),
+            pltpu.SemaphoreType.DMA((4,)),
         ],
-        compiler_params=pltpu.CompilerParams(collective_id=0, has_side_effects=True, vmem_limit_bytes=48 * 2**20),
-    )(field, cells, live, innovations[:, 0], error_weight[:, 0], up_w, down_w)
+        compiler_params=pltpu.CompilerParams(collective_id=0, has_side_effects=True, vmem_limit_bytes=56 * 2**20),
+    )(field, cells, live, innovations[:, 0], error_weight[:, 0], weighting)
 
     def back(state):
         return state.reshape(2, levels, slab, band)

time: 159 us -> 158 us (level)
    unnamed x8 -> x2, local copies, waits for them, and re-layouts: 1.63 us -> 3.79 us
where the time goes in v2:
time: 158 us
  Pallas kernels  151 us (96%)
  local copies, waits for them, and re-layouts  6.01 us (4%)
    pallas_call x1, Pallas kernels, body(): pl.pallas_call(functools.partial(kernel, lon_n, lat_n, levels), out_shape...  151 us
    unnamed x2, local copies, waits for them, and re-layouts  3.79 us

profile of v2, /device:TPU:0, one launch (start us, length us, event | category | flops | bytes accessed | tf_op | source)
XLA Modules:
  0.0 158.0 jit_solution(9333683030073351168)
XLA Ops:
  0.6 1.4 reshape.55.cells
  2.0 0.1 iota.12
  2.1 0.7 lt.20
  2.8 0.1 lt.21
  2.8 0.6 compare_convert_fusion.live
  3.4 150.8 %shard_map.77 = (f32[1096,128]{1,0:T(8,128)}, f32[1096,128]{1,0:T(8,128)}) custom-call(f32[4384,128]{1,0:T(8,128)} %bitcast.9, s32[4,1,128]{2,1,0:T(1,128)} %reshape.55.cells, f32[4,1,128]{2,1,0:T(1,128)} %compare_convert_fusion.live, f32[4,32,4,128]{3,2,1,0:T(4,128)} %bitcast.12, f32[4,32,4,128]{3,2,1,0:T(4,128)} %bitcast.13, f32[274,128]{1,0:T(8,128)} %far_weighting.1), custom_call_target="tpu_custom_call" | custom-call | tf_op jit(solution)/shard_map/pallas_call | solution.py:553
  154.2 1.9 %copy.10 = f32[2,137,4,128]{3,2,1,0:T(4,128)} copy(f32[2,137,4,128]{3,2,1,0:T(4,128)} %bitcast.11) | data formatting | bytes 1122304
  156.1 1.9 %copy.11 = f32[2,137,4,128]{3,2,1,0:T(4,128)} copy(f32[2,137,4,128]{3,2,1,0:T(4,128)} %bitcast.10) | data formatting | bytes 1122304
  (1 shorter events, 0.0 us)
